TPU v7x, 512 devices: a whole 4x8x8 slice. The times are simulated.
512 devices in a mesh: group: 16 (over y, z_hi), member: 32 (over z_lo, x, core).
Axes of the slice: x: 4, y: 8, z: 8 (z_hi: 2, z_lo: 4; z = z_hi * 4 + z_lo), core: 2. Of those that a mesh axis runs over, the one named last changes fastest.
Arguments:
- queries: float32 [4096, 768], P(('group', 'member')), may hold values from -6 to 6
- centroids: float32 [16384, 768], P(('group', 'member')), may hold values from -0.21875 to 0.21875
- stored: float32 [64, 2048, 768], P('group', 'member'), may hold values from -0.21875 to 0.21875
- vector_ids: int32 [64, 2048], P('group', 'member'), may hold values from -1 to 131071, as said below
- list_home: int32 [64], replicated, may hold values from 0 to 63, as said below
- probes: int32 [16, 3, 16], replicated, may hold values from 0 to 63, as said below
Outputs:
- coarse_best: float32 [4096], P(('group', 'member'))
- fine_best: float32 [3, 4096], P(None, ('group', 'member'))
Inputs may be any that keep to these rules, and one draw needn't show every extreme that they name: A permutation: list l is stored at slot list_home[l], and slot t belongs to group t // 4. `probes`: for each block and step the 16 probed lists are stored in 16 different groups, one in each. `vector_ids`: ids are distinct where not -1; each list has its valid vectors first, 256 or more of them.
All inputs are finite; a program needn't handle non-finite values.
Results may differ from a plain program's by a relative error of at most 0.0003.
Values sent between devices are 32-bit elements; how exact they have to be, the bound alone decides.
A program may use at most 64 MiB of HBM per device.

v0:
```python
import jax
import jax.numpy as jnp
from jax import lax
from jax.sharding import PartitionSpec as P

D = 768
STEPS = 3
AXES = ("group", "member")


def local(queries, centroids, stored, vector_ids, list_home, probes):
    member_pos = lax.axis_index("member")
    group_pos = lax.axis_index("group")
    members = lax.axis_size("member")
    rows_dev = queries.shape[0]
    lowest = jnp.float32(-1e30)
    every_query = lax.all_gather(queries, AXES, axis=0, tiled=True)
    lists_here, places = vector_ids.shape
    vectors = stored.reshape(-1, D)

    def score(rows):
        return jnp.einsum(
            "qd,rd->qr", every_query, rows, preferred_element_type=jnp.float32, precision=lax.Precision.HIGH
        )

    coarse = jnp.max(score(centroids), axis=1)
    usable = vector_ids.reshape(-1) >= 0
    fine = jnp.where(usable[None, :], score(vectors), lowest)
    per_list = jnp.max(fine.reshape(-1, lists_here, places), axis=2)

    slot_ids = list_home[probes]
    at_home = slot_ids // lists_here == group_pos
    local_slot = jnp.sum(jnp.where(at_home, slot_ids - group_pos * lists_here, 0), axis=2)
    blocks = local_slot.shape[0]
    chosen = local_slot[:, :, None] == jnp.arange(lists_here)[None, None, :]
    by_block = per_list.reshape(blocks, -1, lists_here)
    steps = [
        jnp.max(jnp.where(chosen[:, s][:, None, :], by_block, lowest), axis=2).reshape(-1) for s in range(STEPS)
    ]
    best = lax.pmax(jnp.stack([coarse] + steps), AXES)
    mine = lax.dynamic_slice_in_dim(best, (group_pos * members + member_pos) * rows_dev, rows_dev, 1)
    return mine[0], mine[1:]


def solution(mesh):
    placed = (
        P(AXES, None),
        P(AXES, None),
        P("group", "member", None),
        P("group", "member"),
        P(),
        P(),
    )
    return jax.shard_map(
        local,
        mesh=mesh,
        in_specs=placed,
        out_specs=(P(AXES), P(None, AXES)),
        check_vma=False,
    )
```

profile of v0, /device:TPU:1, one launch (start us, length us, event | category | flops | bytes accessed | tf_op | source)
XLA Modules:
  0.0 436.6 jit_solution(568290764888922073)
XLA Ops:
  7.2 0.0 copy-start
  7.2 0.0 copy-start.1
  7.2 0.0 all-gather.2.cloned.1.call-start
  7.2 0.7 all-gather.2.cloned.1.call-update
  7.9 0.0 all-reduce.2.cloned.1.call-start
  8.0 0.7 broadcast_compare_fusion
  8.7 0.1 ge.15
  8.8 0.8 compare_select_fusion
  9.5 0.1 reshape.60
  9.6 0.0 copy-done.1
  9.6 4.8 %gather_fusion = s32[768]{0:T(1024)S(1)} fusion(s32[64]{0:T(128)S(1)} %copy-done.1, s32[1024]{0:T(1024)S(1)} %pad_clamp_fusion), kind=kCustom, calls=%fused_computation | custom fusion | bytes 9216 | tf_op jit(solution)/shard_map/gather | solution.py:31
  14.4 0.0 copy-start.2
  14.4 0.1 reshape.59
  14.5 0.4 select_reduce_fusion
  14.9 0.1 copy.20
  15.0 134.6 %all-gather.2.cloned.1.call-done = f32[4096,768]{1,0:T(8,128)} async-done(((f32[8,768]{1,0:T(8,128)}), f32[4096,768]{1,0:T(8,128)}) %all-gather.2.cloned.1.call-update) | async-done | bytes 12582928 | tf_op jit(solution)/shard_map/all_gather | solution.py:17
  149.5 0.0 copy-done
  149.5 0.0 slice-start
  149.6 0.0 slice-start.1
  149.6 0.0 slice-start.2
  149.6 17.4 %bitcast_reduce_fusion = f32[4096,4]{0,1:T(4,128)S(1)} fusion(f32[4096,768]{1,0:T(8,128)} %all-gather.2.cloned.1.call-done, f32[256,768]{1,0:T(8,128)S(1)} %bitcast.38, pred[256]{0:T(512)(128)(4,1)S(1)} %ge.15), kind=kOutput, calls=%fused_computation.2 | convolution fusion | flops 4833918976 | bytes 13435136 | tf_op jit(solution)/shard_map/qd,rd->qr/dot_general | solution.py:22
  167.0 0.1 fusion
  167.1 0.0 copy-done.2
  167.1 0.0 slice-done
  167.2 0.0 slice-done.1
  167.2 0.0 slice-done.2
  167.2 5.5 %convolution_reduce_fusion = f32[4096]{0:T(1024)S(1)} fusion(f32[4096,768]{1,0:T(8,128)S(1)} %bitcast.40, f32[32,768]{1,0:T(8,128)S(1)} %copy-done.2), kind=kOutput, calls=%fused_computation.3 | convolution fusion | flops 604106752 | bytes 12697600 | tf_op jit(solution)/shard_map/qd,rd->qr/dot_general | solution.py:22
  172.7 0.7 pad_maximum_fusion
  173.4 0.0 all-reduce.2.cloned.1.call-update
  173.4 254.4 %all-reduce.2.cloned.1.call-done = f32[4,4096]{1,0:T(4,128)} async-done(((f32[4,4096]{1,0:T(4,128)}), f32[4,4096]{1,0:T(4,128)}) %all-reduce.2.cloned.1.call-update) | async-done | bytes 65552 | tf_op jit(solution)/shard_map/pmax | solution.py:40
  427.9 0.8 constant_dynamic-slice_fusion
  428.6 0.5 slice_bitcast_fusion.3
  429.2 0.6 slice.19
  (7 shorter events, 0.1 us)
Async XLA Ops:
  7.2 142.4 %copy-start = (f32[4,64,768]{2,1,0:T(8,128)S(1)}, f32[4,64,768]{2,1,0:T(8,128)}, u32[]{:S(2)}) copy-start(f32[4,64,768]{2,1,0:T(8,128)} %param.8) | copy-start | bytes 2359300
  7.2 2.4 copy-start.1
  7.2 142.4 %all-gather.2.cloned.1.call-start = ((), (), s32[]{:S(2)}) async-start(), calls=%async_computation | async-start | bytes 12607488 | tf_op jit(solution)/shard_map/all_gather | solution.py:17
  7.9 420.0 %all-reduce.2.cloned.1.call-start = ((), (), s32[]{:S(2)}) async-start(), calls=%async_computation.1 | async-start | bytes 131072 | tf_op jit(solution)/shard_map/pmax | solution.py:40
  14.4 152.7 %copy-start.2 = (f32[32,768]{1,0:T(8,128)S(1)}, f32[32,768]{1,0:T(8,128)}, u32[]{:S(2)}) copy-start(f32[32,768]{1,0:T(8,128)} %param.7) | copy-start | bytes 294916
  149.5 17.6 %slice-start = ((s8[12582912]{0:T(1024)(128)(4,1)}), s8[4194304]{0:T(1024)(128)(4,1)S(1)}, s32[]{:S(2)}) async-start(s8[12582912]{0:T(1024)(128)(4,1)} %bitcast.39), calls=%async_computation.2 | async-start | bytes 8388608
  149.6 17.6 %slice-start.1 = ((s8[12582912]{0:T(1024)(128)(4,1)}), s8[4194304]{0:T(1024)(128)(4,1)S(1)}, s32[]{:S(2)}) async-start(s8[12582912]{0:T(1024)(128)(4,1)} %bitcast.39), calls=%async_computation.3 | async-start | bytes 8388608
  149.6 17.6 %slice-start.2 = ((s8[12582912]{0:T(1024)(128)(4,1)}), s8[4194304]{0:T(1024)(128)(4,1)S(1)}, s32[]{:S(2)}) async-start(s8[12582912]{0:T(1024)(128)(4,1)} %bitcast.39), calls=%async_computation.4 | async-start | bytes 8388608
Sparse Core Ops, SparseCore 0:
  12.5 137.0 all-gather.1
  173.6 254.2 all-reduce.1
where the time goes:
time: 437 us
  waiting for transfers between devices  390 us (89%)
  matrix products  22.9 us (5%)
  between operations  14.2 us (3%)
  local copies, waits for them, and re-layouts  7.06 us (2%)
    pmax x1, waiting for transfers between devices, local(): best = lax.pmax(jnp.stack([coarse] + steps), AXES)  254 us
    all_gather x1, waiting for transfers between devices, local(): every_query = lax.all_gather(queries, AXES, axis=0, tiled=True)  135 us
    dot_general x2, matrix products, score(): jnp.einsum('qd,rd->qr', every_query, rows, preferred_element_type=jnp.flo...  22.9 us
  transfers between devices with their start and end apart: 2, of which 2 were waited for; matrix products, arithmetic and copies ran while one was open for 2% of the time, Pallas kernels for 0%

commit v1 on v0

v1 whole, which is shorter than its diff:
```python
import jax
import jax.numpy as jnp
from jax import lax
from jax.experimental import pallas as pl
from jax.experimental.pallas import tpu as pltpu
from jax.sharding import PartitionSpec as P

D = 768
STEPS = 3
AXES = ("group", "member")
LOW = -1e30
NX, NY, NZ, ZL = 4, 8, 8, 4
PART = D // 3
SIZES = (NX, NY, NZ)
X, Y, Z = 0, 1, 2
ORDERS = ((X, Y, Z), (Y, Z, X), (Z, X, Y))
VMEM_SPEC = pl.BlockSpec(memory_space=pltpu.VMEM)


def place():
    g, m = lax.axis_index("group"), lax.axis_index("member")
    x, y, core = (m // 2) % NX, g // 2, m % 2
    z = (g % 2) * ZL + m // (2 * NX)
    return [x, y, z], core


def device(at, core):
    x, y, z = at
    return (y * 2 + z // ZL, (z % ZL) * (2 * NX) + x * 2 + core)


def moved(at, axis, steps):
    size = SIZES[axis]
    out = list(at)
    out[axis] = lax.rem(at[axis] + (steps + size), size)
    return out


def greet(at, core):
    barrier = pltpu.get_barrier_semaphore()
    peers = [device(moved(at, axis, d), core) for axis in (X, Y, Z) for d in range(1, SIZES[axis])]
    return barrier, peers


def meet(barrier, peers):
    for peer in peers:
        pl.semaphore_signal(barrier, inc=1, device_id=peer, device_id_type=pl.DeviceIdType.MESH)
    pl.semaphore_wait(barrier, len(peers))


def gather_kernel(q, cent, stored, bias, out, cent_in, stored_in, bias_in, sends, recvs, local_sems):
    at, core = place()
    barrier, peers = greet(at, core)
    partner = device(at, 1 - core)
    meet(barrier, peers + [partner])
    used = [0]
    started = []

    def send(src, dst, to, sem):
        copy = pltpu.make_async_remote_copy(
            src_ref=src,
            dst_ref=dst,
            send_sem=sends.at[sem],
            recv_sem=recvs.at[sem],
            device_id=to,
            device_id_type=pl.DeviceIdType.MESH,
        )
        copy.start()
        started.append(copy)

    def arrived(slot, sem):
        pltpu.make_async_remote_copy(
            src_ref=slot,
            dst_ref=slot,
            send_sem=sends.at[sem],
            recv_sem=recvs.at[sem],
            device_id=partner,
            device_id_type=pl.DeviceIdType.MESH,
        ).wait_recv()

    def new_sem():
        used[0] += 1
        return used[0] - 1

    def columns(part):
        return q.at[:, pl.ds(part * PART, PART)]

    firsts = []
    for part, order in enumerate(ORDERS):
        mine = []
        for d in range(1, SIZES[order[0]]):
            sem = new_sem()
            slot = out.at[part, at[Z], at[Y], at[X]]
            send(columns(part), slot, device(moved(at, order[0], d), core), sem)
            fx, fy, fz = moved(at, order[0], -d)
            mine.append((out.at[part, fz, fy, fx], sem))
        firsts.append(mine)
    own = []
    for part in range(3):
        copy = pltpu.make_async_copy(columns(part), out.at[part, at[Z], at[Y], at[X]], local_sems.at[part])
        copy.start()
        own.append(copy)
    swaps = []
    for src, dst in ((stored, stored_in), (cent, cent_in), (bias, bias_in)):
        sem = new_sem()
        send(src, dst, partner, sem)
        swaps.append((dst, sem))

    def slab(part, phase, pos, half):
        x, y, z = at
        first = pl.ds(0 if half == 0 else (2 if (part, phase) == (0, 1) else 4), 2 if (part, phase) == (0, 1) else 4)
        if part == 0:
            return out.at[0, z, pos, first] if phase == 1 else out.at[0, pos, first]
        if part == 1:
            return out.at[1, pos, first, x] if phase == 1 else out.at[1, first, :, pos]
        return out.at[2, first, y, pos] if phase == 1 else out.at[2, first, pos]

    def ring(part, phase):
        axis = ORDERS[part][phase]
        size = SIZES[axis]
        last = size // 2
        streams = []
        for way in (1, -1):
            for turn in (0, 1):
                half = turn if way == 1 else 1 - turn
                hops = last if turn == 0 else last - 1
                streams.append((way, turn, half, hops, [new_sem() for _ in range(hops)]))

        def pos(offset):
            return lax.rem(at[axis] + (offset + size), size)

        def hop(stream, step):
            way, turn, half, hops, sems = stream
            piece = slab(part, phase, pos(-way * step), half)
            send(piece, piece, device(moved(at, axis, way), core), sems[step])

        def take(stream, step):
            way, turn, half, hops, sems = stream
            arrived(slab(part, phase, pos(-way * (step + 1)), half), sems[step])

        for turn in (0, 1):
            for stream in streams:
                if stream[1] == turn:
                    hop(stream, 0)
        if size == NX:
            yield
        for step in range(last):
            for turn in (0, 1):
                yield
                for stream in streams:
                    if stream[1] == turn and step < stream[3]:
                        take(stream, step)
                        if step + 1 < stream[3]:
                            hop(stream, step + 1)

    def whole(part):
        own[part].wait()
        for slot, sem in firsts[part]:
            arrived(slot, sem)
        yield from ring(part, 1)
        yield from ring(part, 2)

    running = [whole(0), whole(2), whole(1)]
    while running:
        for item in list(running):
            try:
                next(item)
            except StopIteration:
                running.remove(item)
    for slot, sem in swaps:
        arrived(slot, sem)
    for copy in started:
        copy.wait_send()


def score_kernel(g, st, st_in, ce, ce_in, bias, bias_in, chosen, out, high, low, base):
    lists = 4
    rows = st.shape[0]
    places = rows // lists
    cents = ce.shape[0]

    @pl.when(pl.program_id(0) == 0)
    def _():
        start = 0
        for ref in (st, st_in, ce, ce_in):
            count = ref.shape[0]
            top = ref[...].astype(jnp.bfloat16)
            high[start : start + count, :] = top
            low[start : start + count, :] = (ref[...] - top.astype(jnp.float32)).astype(jnp.bfloat16)
            start += count
        base[:rows, :128] = bias[...]
        base[:rows, 128:] = bias[...]
        base[rows : 2 * rows, :128] = bias_in[...]
        base[rows : 2 * rows, 128:] = bias_in[...]
        base[2 * rows :, :] = jnp.zeros((2 * cents, 256), jnp.float32)

    def dot(a, b):
        return lax.dot_general(a, b, (((1,), (1,)), ((), ())), preferred_element_type=jnp.float32)

    total = base[...]
    for part in range(3):
        q = g[part, 0].reshape(NY * NX * 8, PART)
        q_high = q.astype(jnp.bfloat16)
        q_low = (q - q_high.astype(jnp.float32)).astype(jnp.bfloat16)
        v_high = high[:, part * PART : (part + 1) * PART]
        v_low = low[:, part * PART : (part + 1) * PART]
        total = total + (dot(v_high, q_high) + (dot(v_high, q_low) + dot(v_low, q_high)))
    best = []
    for i in range(lists):
        a = jnp.max(total[i * places : (i + 1) * places], axis=0, keepdims=True)
        b = jnp.max(total[rows + i * places : rows + (i + 1) * places], axis=0, keepdims=True)
        best.append(jnp.maximum(a, b))
    out[0, 0:1, :] = jnp.max(total[2 * rows :], axis=0, keepdims=True)
    for s in range(STEPS):
        top = best[0] + chosen[0, s * lists : s * lists + 1, :]
        for i in range(1, lists):
            top = jnp.maximum(top, best[i] + chosen[0, s * lists + i : s * lists + i + 1, :])
        out[0, s + 1 : s + 2, :] = top


def reduce_kernel(part, out, from_z, from_x, from_y, mid_z, mid_x, sends, recvs):
    at, core = place()
    barrier, peers = greet(at, core)
    meet(barrier, peers)
    used = 0

    def swap(axis, source, landing, first):
        copies = []
        for d in range(1, SIZES[axis]):
            copy = pltpu.make_async_remote_copy(
                src_ref=source(d),
                dst_ref=landing.at[d - 1],
                send_sem=sends.at[first + d - 1],
                recv_sem=recvs.at[first + d - 1],
                device_id=device(moved(at, axis, d), core),
                device_id_type=pl.DeviceIdType.MESH,
            )
            copy.start()
            copies.append(copy)
        for copy in copies:
            copy.wait()

    def most(value, landing):
        for i in range(landing.shape[0]):
            value = jnp.maximum(value, landing[i])
        return value

    swap(Z, lambda d: part.at[lax.rem(at[Z] + d, NZ)], from_z, 0)
    mid_z[...] = most(part[at[Z]], from_z)
    swap(X, lambda d: mid_z, from_x, NZ - 1)
    mid_x[...] = most(mid_z[...], from_x)
    swap(Y, lambda d: mid_x, from_y, NZ + NX - 2)
    out[...] = most(mid_x[...], from_y)


def local(queries, centroids, stored, vector_ids, list_home, probes):
    (x, y, z), core = place()
    group_pos = lax.axis_index("group")
    lists, places = vector_ids.shape
    rows = lists * places
    cents = centroids.shape[0]
    f32 = jnp.float32
    vectors = stored.reshape(rows, D)
    bias = jnp.where(vector_ids.reshape(rows, 1) >= 0, f32(0), f32(LOW))
    bias = jnp.broadcast_to(bias, (rows, 128))

    slot_ids = list_home[probes]
    at_home = slot_ids // lists == group_pos
    local_slot = jnp.sum(jnp.where(at_home, slot_ids - group_pos * lists, 0), axis=2)
    chosen = local_slot[:, :, None] == jnp.arange(lists)[None, None, :]
    chosen = jnp.where(chosen, f32(0), f32(LOW)).reshape(NY, 2, STEPS * lists)
    chosen = jnp.transpose(chosen, (1, 2, 0))[:, None, :, :, None]
    chosen = jnp.broadcast_to(chosen, (2, ZL, STEPS * lists, NY, NX * 8)).reshape(NZ, STEPS * lists, NY * NX * 8)

    everything = (3, NZ, NY, NX, 8, PART)
    copies = 17 + 3 + 2 * 34
    gathered, cent_in, stored_in, bias_in = pl.pallas_call(
        gather_kernel,
        out_shape=[
            jax.ShapeDtypeStruct(everything, f32),
            jax.ShapeDtypeStruct((cents, D), f32),
            jax.ShapeDtypeStruct((rows, D), f32),
            jax.ShapeDtypeStruct((rows, 128), f32),
        ],
        in_specs=[VMEM_SPEC] * 4,
        out_specs=[VMEM_SPEC] * 4,
        scratch_shapes=[
            pltpu.SemaphoreType.DMA((copies,)),
            pltpu.SemaphoreType.DMA((copies,)),
            pltpu.SemaphoreType.DMA((3,)),
        ],
        compiler_params=pltpu.CompilerParams(collective_id=0, has_side_effects=True, vmem_limit_bytes=40 << 20),
        name="gather",
    )(queries, centroids, vectors, bias)

    def fixed(*shape):
        return pl.BlockSpec(shape, lambda i: (0,) * len(shape))

    partial = pl.pallas_call(
        score_kernel,
        grid=(NZ,),
        out_shape=jax.ShapeDtypeStruct((NZ, 1 + STEPS, NY * NX * 8), f32),
        in_specs=[
            pl.BlockSpec((3, 1, NY, NX, 8, PART), lambda i: (0, i, 0, 0, 0, 0)),
            fixed(rows, D),
            fixed(rows, D),
            fixed(cents, D),
            fixed(cents, D),
            fixed(rows, 128),
            fixed(rows, 128),
            pl.BlockSpec((1, STEPS * lists, NY * NX * 8), lambda i: (i, 0, 0)),
        ],
        out_specs=pl.BlockSpec((1, 1 + STEPS, NY * NX * 8), lambda i: (i, 0, 0)),
        scratch_shapes=[
            pltpu.VMEM((2 * rows + 2 * cents, D), jnp.bfloat16),
            pltpu.VMEM((2 * rows + 2 * cents, D), jnp.bfloat16),
            pltpu.VMEM((2 * rows + 2 * cents, 256), f32),
        ],
        compiler_params=pltpu.CompilerParams(vmem_limit_bytes=40 << 20),
        name="score",
    )(gathered, vectors, stored_in, centroids, cent_in, bias, bias_in, chosen)

    piece = (1 + STEPS, NY * NX * 8)
    best = pl.pallas_call(
        reduce_kernel,
        out_shape=jax.ShapeDtypeStruct(piece, f32),
        in_specs=[VMEM_SPEC],
        out_specs=VMEM_SPEC,
        scratch_shapes=[
            pltpu.VMEM((NZ - 1,) + piece, f32),
            pltpu.VMEM((NX - 1,) + piece, f32),
            pltpu.VMEM((NY - 1,) + piece, f32),
            pltpu.VMEM(piece, f32),
            pltpu.VMEM(piece, f32),
            pltpu.SemaphoreType.DMA((NX + NY + NZ - 3,)),
            pltpu.SemaphoreType.DMA((NX + NY + NZ - 3,)),
        ],
        compiler_params=pltpu.CompilerParams(collective_id=1, has_side_effects=True),
        name="reduce",
    )(partial)
    mine = lax.dynamic_slice_in_dim(best, (y * NX + x) * 8, 8, 1)
    return mine[0], mine[1:]


def solution(mesh):
    placed = (
        P(AXES, None),
        P(AXES, None),
        P("group", "member", None),
        P("group", "member"),
        P(),
        P(),
    )
    return jax.shard_map(
        local,
        mesh=mesh,
        in_specs=placed,
        out_specs=(P(AXES), P(None, AXES)),
        check_vma=False,
    )
```

time: 437 us -> 95.9 us (0.22)
  the two profiles are of different devices: /device:TPU:1 before, /device:TPU:8 now
where the time goes in v1:
time: 95.9 us; the launch traced here: 95.6 us
  Pallas kernels  84.7 us (88%)
  local copies, waits for them, and re-layouts  8.24 us (9%)
  other arithmetic  1.81 us (2%)
    pallas_call x1, Pallas kernels, local(): pl.pallas_call(gather_kernel, out_shape=[jax.ShapeDtypeStruct(everything,...  58.4 us
    pallas_call x1, Pallas kernels, local(): pl.pallas_call(reduce_kernel, out_shape=jax.ShapeDtypeStruct(piece, f32),...  18.3 us
    pallas_call x1, Pallas kernels, local(): pl.pallas_call(score_kernel, grid=(NZ,), out_shape=jax.ShapeDtypeStruct((...  8.05 us
    gather x2, local copies, waits for them, and re-layouts, local(): slot_ids = list_home[probes]  4.87 us

profile of v1, /device:TPU:8, one launch (start us, length us, event | category | flops | bytes accessed | tf_op | source)
XLA Modules:
  0.0 95.6 jit_solution(1819672918059626385)
XLA Ops:
  0.6 0.0 copy-start
  0.7 0.7 compare_select_fusion.2
  1.4 0.1 select_n.47
  1.5 0.1 eq.33
  1.6 0.8 compare_select_fusion
  2.3 0.1 reshape.34
  2.4 0.0 copy-done
  2.4 0.0 copy-start.1
  2.4 0.0 copy-start.2
  2.4 0.0 copy-start.4
  2.5 4.8 %gather_fusion = s32[768]{0:T(1024)S(1)} fusion(s32[64]{0:T(128)S(1)} %copy-done, s32[1024]{0:T(1024)S(1)} %pad_clamp_fusion), kind=kCustom, calls=%fused_computation | custom fusion | bytes 9216 | tf_op jit(solution)/shard_map/gather | solution.py:267
  7.2 0.1 reshape.33
  7.3 0.4 select_reduce_fusion
  7.7 0.1 eq.30
  7.8 0.1 eq.31
  7.9 0.1 copy.11
  8.0 0.1 broadcast_in_dim.36.bias
  8.1 0.1 broadcast_in_dim.40
  8.2 0.2 reshape.31
  8.4 0.0 copy-done.1
  8.4 0.0 copy-done.2
  8.4 0.0 copy-done.4
  8.4 58.4 %gather.7 = (f32[3,8,8,4,8,256]{5,4,3,2,1,0:T(8,128)S(1)}, f32[32,768]{1,0:T(8,128)S(1)}, f32[256,768]{1,0:T(8,128)S(1)}, f32[256,128]{1,0:T(8,128)S(1)}) custom-call(f32[8,768]{1,0:T(8,128)S(1)} %copy-done.4, f32[32,768]{1,0:T(8,128)S(1)} %copy-done.2, f32[256,768]{1,0:T(8,128)S(1)} %bitcast.9, f32[256,128]{1,0:T(8,128)S(1)} %broadcast_in_dim.36.bias), custom_call_target="tpu_custom_call" | custom-call | tf_op jit(solution)/shard_map/gather/pallas_call | solution.py:277
  66.8 8.1 %score.1.part = f32[8,4,256]{2,1,0:T(4,128)S(1)} custom-call(f32[3,8,8,4,8,256]{5,4,3,2,1,0:T(8,128)S(1)} %get-tuple-element.6.g, f32[256,768]{1,0:T(8,128)S(1)} %bitcast.10, f32[256,768]{1,0:T(8,128)S(1)} %get-tuple-element.7.st_in, f32[32,768]{1,0:T(8,128)S(1)} %copy-done.2, f32[32,768]{1,0:T(8,128)S(1)} %get-tuple-element.8.ce_in, ...), custom_call_target="tpu_custom_call" | custom-call | tf_op jit(solution)/shard_map/score/pallas_call | solution.py:299
  74.8 0.0 copy-start.3
  74.8 0.6 copy-done.3
  75.4 18.3 %reduce.1 = f32[4,256]{1,0:T(4,128)} custom-call(f32[8,4,256]{2,1,0:T(4,128)} %copy-done.3), custom_call_target="tpu_custom_call" | custom-call | tf_op jit(solution)/shard_map/reduce/pallas_call | solution.py:324
  93.8 0.8 constant_dynamic-slice_fusion
  94.5 0.5 slice_bitcast_fusion
  95.0 0.6 slice.7
  (4 shorter events, 0.1 us)
Async XLA Ops:
  0.6 1.8 %copy-start = (s32[64]{0:T(128)S(1)}, s32[64]{0:T(128)}, u32[]{:S(2)}) copy-start(s32[64]{0:T(128)} %param.10) | copy-start | bytes 772
  2.4 6.0 %copy-start.1 = (f32[4,64,768]{2,1,0:T(8,128)S(1)}, f32[4,64,768]{2,1,0:T(8,128)}, u32[]{:S(2)}) copy-start(f32[4,64,768]{2,1,0:T(8,128)} %param.8) | copy-start | bytes 2359300
  2.4 6.0 %copy-start.2 = (f32[32,768]{1,0:T(8,128)S(1)}, f32[32,768]{1,0:T(8,128)}, u32[]{:S(2)}) copy-start(f32[32,768]{1,0:T(8,128)} %ce.1) | copy-start | bytes 294916
  2.4 6.0 %copy-start.4 = (f32[8,768]{1,0:T(8,128)S(1)}, f32[8,768]{1,0:T(8,128)}, u32[]{:S(2)}) copy-start(f32[8,768]{1,0:T(8,128)} %q.1) | copy-start | bytes 73732
  74.8 0.6 copy-start.3

commit v2 on v1

v2 whole, which is shorter than its diff:
```python
import jax
import jax.numpy as jnp
from jax import lax
from jax.experimental import pallas as pl
from jax.experimental.pallas import tpu as pltpu
from jax.sharding import PartitionSpec as P

D = 768
STEPS = 3
AXES = ("group", "member")
LOW = -1e30
NX, NY, NZ, ZL = 4, 8, 8, 4
PART = D // 3
SIZES = (NX, NY, NZ)
X, Y, Z = 0, 1, 2
ORDERS = ((X, Y, Z), (Y, Z, X), (Z, X, Y))
VMEM_SPEC = pl.BlockSpec(memory_space=pltpu.VMEM)


def place():
    g, m = lax.axis_index("group"), lax.axis_index("member")
    x, y, core = (m // 2) % NX, g // 2, m % 2
    z = (g % 2) * ZL + m // (2 * NX)
    return [x, y, z], core


def device(at, core):
    x, y, z = at
    return (y * 2 + z // ZL, (z % ZL) * (2 * NX) + x * 2 + core)


def moved(at, axis, steps):
    size = SIZES[axis]
    out = list(at)
    out[axis] = lax.rem(at[axis] + (steps + size), size)
    return out


def greet(at, core):
    barrier = pltpu.get_barrier_semaphore()
    peers = [device(moved(at, axis, d), core) for axis in (X, Y, Z) for d in range(1, SIZES[axis])]
    return barrier, peers


def meet(barrier, peers):
    for peer in peers:
        pl.semaphore_signal(barrier, inc=1, device_id=peer, device_id_type=pl.DeviceIdType.MESH)
    pl.semaphore_wait(barrier, len(peers))


def kernel(q, cent, stored, ids, home, probes, best, out, cent_in, stored_in, ids_in, high, low, base, pick, acc,
           partial, from_z, from_x, from_y, mid_z, mid_x, sends, recvs, local_sems):
    at, core = place()
    group = lax.axis_index("group")
    lists, places = ids.shape
    rows = lists * places
    cents = cent.shape[0]
    width = NY * NX * 8
    barrier, peers = greet(at, core)
    partner = device(at, 1 - core)
    meet(barrier, peers + [partner])
    used = [0]
    started = []

    def send(src, dst, to, sem):
        copy = pltpu.make_async_remote_copy(
            src_ref=src,
            dst_ref=dst,
            send_sem=sends.at[sem],
            recv_sem=recvs.at[sem],
            device_id=to,
            device_id_type=pl.DeviceIdType.MESH,
        )
        copy.start()
        return copy

    def arrived(slot, sem):
        pltpu.make_async_remote_copy(
            src_ref=slot,
            dst_ref=slot,
            send_sem=sends.at[sem],
            recv_sem=recvs.at[sem],
            device_id=partner,
            device_id_type=pl.DeviceIdType.MESH,
        ).wait_recv()

    def new_sem(count=1):
        used[0] += count
        return used[0] - count

    def columns(part):
        return q.at[:, pl.ds(part * PART, PART)]

    firsts = []
    for part, order in enumerate(ORDERS):
        mine = []
        for d in range(1, SIZES[order[0]]):
            sem = new_sem()
            slot = out.at[part, at[Z], at[Y], at[X]]
            started.append(send(columns(part), slot, device(moved(at, order[0], d), core), sem))
            fx, fy, fz = moved(at, order[0], -d)
            mine.append((out.at[part, fz, fy, fx], sem))
        firsts.append(mine)
    own = []
    for part in range(3):
        copy = pltpu.make_async_copy(columns(part), out.at[part, at[Z], at[Y], at[X]], local_sems.at[part])
        copy.start()
        own.append(copy)
    swaps = []
    for src, dst in ((stored, stored_in), (cent, cent_in), (ids, ids_in)):
        sem = new_sem()
        started.append(send(src, dst, partner, sem))
        swaps.append((dst, sem))

    def slab(part, phase, pos, half):
        x, y, z = at
        first = pl.ds(0 if half == 0 else (2 if (part, phase) == (0, 1) else 4), 2 if (part, phase) == (0, 1) else 4)
        if part == 0:
            return out.at[0, z, pos, first] if phase == 1 else out.at[0, pos, first]
        if part == 1:
            return out.at[1, pos, first, x] if phase == 1 else out.at[1, first, :, pos]
        return out.at[2, first, y, pos] if phase == 1 else out.at[2, first, pos]

    def ring(part, phase, filled=None):
        axis = ORDERS[part][phase]
        size = SIZES[axis]
        last = size // 2
        streams = []
        for way in (1, -1):
            for turn in (0, 1):
                half = turn if way == 1 else 1 - turn
                hops = last if turn == 0 else last - 1
                streams.append((way, turn, half, hops, [new_sem() for _ in range(hops)]))

        def pos(offset):
            return lax.rem(at[axis] + (offset + size), size)

        def hop(stream, step):
            way, turn, half, hops, sems = stream
            piece = slab(part, phase, pos(-way * step), half)
            started.append(send(piece, piece, device(moved(at, axis, way), core), sems[step]))

        def take(stream, step):
            way, turn, half, hops, sems = stream
            arrived(slab(part, phase, pos(-way * (step + 1)), half), sems[step])

        for turn in (0, 1):
            for stream in streams:
                if stream[1] == turn:
                    hop(stream, 0)
        if size == NX:
            yield
        for step in range(last):
            for turn in (0, 1):
                yield
                for stream in streams:
                    if stream[1] == turn and step < stream[3]:
                        take(stream, step)
                        if step + 1 < stream[3]:
                            hop(stream, step + 1)
            if filled is not None:
                filled(step)

    def dot(a, b):
        return lax.dot_general(a, b, (((1,), (1,)), ((), ())), preferred_element_type=jnp.float32)

    def product(part, z):
        rhs = out[part, z].reshape(width, PART)
        rhs_high = rhs.astype(jnp.bfloat16)
        rhs_low = (rhs - rhs_high.astype(jnp.float32)).astype(jnp.bfloat16)
        v_high = high[:, part * PART : (part + 1) * PART]
        v_low = low[:, part * PART : (part + 1) * PART]
        return dot(v_high, rhs_high) + (dot(v_high, rhs_low) + dot(v_low, rhs_high))

    def prepare_vectors():
        for slot, sem in swaps:
            arrived(slot, sem)
        start = 0
        for ref in (stored, stored_in, cent, cent_in):
            count = ref.shape[0]
            top = ref[...].astype(jnp.bfloat16)
            high[start : start + count, :] = top
            low[start : start + count, :] = (ref[...] - top.astype(jnp.float32)).astype(jnp.bfloat16)
            start += count
        across = lax.broadcasted_iota(jnp.int32, (places, places), 1)
        down = lax.broadcasted_iota(jnp.int32, (places, places), 0)
        for n, ref in enumerate((ids, ids_in)):
            for i in range(lists):
                row = jnp.where(ref[i : i + 1, :] >= 0, jnp.float32(0), jnp.float32(LOW))
                column = jnp.sum(jnp.where(across == down, row, jnp.float32(0)), axis=1, keepdims=True)
                first = n * rows + i * places
                base[first : first + places, :] = jnp.broadcast_to(column, (places, width))
        base[2 * rows :, :] = jnp.zeros((2 * cents, width), jnp.float32)

    def prepare_picks():
        at_slot = lax.broadcasted_iota(jnp.int32, home.shape, 1)
        row = lax.broadcasted_iota(jnp.int32, (probes.shape[0], width), 0)
        y_of = lax.broadcasted_iota(jnp.int32, (probes.shape[0], width), 1) // (NX * 8)
        for i in range(lists):
            held = jnp.max(jnp.where(home[...] == group * lists + i, at_slot, -1), axis=1, keepdims=True)
            hit = jnp.where(probes[...] == held, jnp.float32(0), jnp.float32(LOW))
            hit = jnp.max(hit, axis=1, keepdims=True)
            for zh in range(2):
                for s in range(STEPS):
                    here = row == (y_of * 2 + zh) * STEPS + s
                    line = jnp.where(here, hit, jnp.float32(LOW))
                    pick[zh, s * lists + i : s * lists + i + 1, :] = jnp.max(line, axis=0, keepdims=True)

    def first_third(begin, stride, count):
        def one(k, _):
            z = lax.rem(at[Z] + (begin + NZ + k * stride), NZ)
            acc[z] = base[...] + product(0, z)
            return 0

        lax.fori_loop(0, count, one, 0)

    def filled(step):
        if step == 0:
            first_third(-1, 1, 3)
        elif step < NZ // 2 - 1:
            first_third(-(step + 1), 2 * (step + 1), 2)
        else:
            first_third(NZ // 2, 1, 1)

    def whole(part):
        own[part].wait()
        for slot, sem in firsts[part]:
            arrived(slot, sem)
        yield from ring(part, 1)
        yield from ring(part, 2, filled if part == 0 else None)

    prepare_picks()
    running = [whole(0), whole(2), whole(1)]
    turns = 0
    while running:
        for item in list(running):
            try:
                next(item)
            except StopIteration:
                running.remove(item)
        turns += 1
        if turns == 4:
            prepare_vectors()

    first_z = new_sem(NZ)

    def z_copy(d):
        return pltpu.make_async_remote_copy(
            src_ref=partial.at[lax.rem(at[Z] + d, NZ)],
            dst_ref=from_z.at[d - 1],
            send_sem=sends.at[first_z + d],
            recv_sem=recvs.at[first_z + d],
            device_id=device(moved(at, Z, d), core),
            device_id_type=pl.DeviceIdType.MESH,
        )

    def distance(k):
        return NZ // 2 + ((k + 1) // 2) * (1 - 2 * (k % 2))

    def finish(k, _):
        @pl.when(k > 0)
        def _():
            z_copy(distance(k - 1)).start()

        z = lax.rem(at[Z] + distance(k), NZ)
        total = acc[z] + (product(1, z) + product(2, z))
        tops = []
        for i in range(lists):
            a = jnp.max(total[i * places : (i + 1) * places], axis=0, keepdims=True)
            b = jnp.max(total[rows + i * places : rows + (i + 1) * places], axis=0, keepdims=True)
            tops.append(jnp.maximum(a, b))
        partial[z, 0:1, :] = jnp.max(total[2 * rows :], axis=0, keepdims=True)
        chosen = pick[z // ZL]
        for s in range(STEPS):
            top = tops[0] + chosen[s * lists : s * lists + 1, :]
            for i in range(1, lists):
                top = jnp.maximum(top, tops[i] + chosen[s * lists + i : s * lists + i + 1, :])
            partial[z, s + 1 : s + 2, :] = top
        return 0

    lax.fori_loop(0, NZ, finish, 0)

    def most(value, landing):
        for i in range(landing.shape[0]):
            value = jnp.maximum(value, landing[i])
        return value

    def swap(axis, source, landing):
        copies = []
        for d in range(1, SIZES[axis]):
            copies.append(send(source, landing.at[d - 1], device(moved(at, axis, d), core), new_sem()))
        for copy in copies:
            copy.wait()

    for d in range(1, NZ):
        z_copy(d).wait()
    mid_z[...] = most(partial[at[Z]], from_z)
    swap(X, mid_z, from_x)
    mid_x[...] = most(mid_z[...], from_x)
    swap(Y, mid_x, from_y)
    best[...] = most(mid_x[...], from_y)
    for copy in started:
        copy.wait_send()


def local(queries, centroids, stored, vector_ids, list_home, probes):
    (x, y, z), core = place()
    lists, places = vector_ids.shape
    rows = lists * places
    cents = centroids.shape[0]
    f32 = jnp.float32
    width = NY * NX * 8
    piece = (1 + STEPS, width)
    held = 2 * rows + 2 * cents
    copies = 17 + 3 + 2 * 34 + NZ + NX + NY - 2
    best = pl.pallas_call(
        kernel,
        out_shape=jax.ShapeDtypeStruct(piece, f32),
        in_specs=[VMEM_SPEC] * 6,
        out_specs=VMEM_SPEC,
        scratch_shapes=[
            pltpu.VMEM((3, NZ, NY, NX, 8, PART), f32),
            pltpu.VMEM((cents, D), f32),
            pltpu.VMEM((rows, D), f32),
            pltpu.VMEM((lists, places), jnp.int32),
            pltpu.VMEM((held, D), jnp.bfloat16),
            pltpu.VMEM((held, D), jnp.bfloat16),
            pltpu.VMEM((held, width), f32),
            pltpu.VMEM((2, STEPS * lists, width), f32),
            pltpu.VMEM((NZ, held, width), f32),
            pltpu.VMEM((NZ,) + piece, f32),
            pltpu.VMEM((NZ - 1,) + piece, f32),
            pltpu.VMEM((NX - 1,) + piece, f32),
            pltpu.VMEM((NY - 1,) + piece, f32),
            pltpu.VMEM(piece, f32),
            pltpu.VMEM(piece, f32),
            pltpu.SemaphoreType.DMA((copies,)),
            pltpu.SemaphoreType.DMA((copies,)),
            pltpu.SemaphoreType.DMA((3,)),
        ],
        compiler_params=pltpu.CompilerParams(collective_id=0, has_side_effects=True, vmem_limit_bytes=48 << 20),
        name="search",
    )(queries, centroids, stored.reshape(rows, D), vector_ids, list_home.reshape(1, -1), probes.reshape(-1, probes.shape[2]))
    mine = lax.dynamic_slice_in_dim(best, (y * NX + x) * 8, 8, 1)
    return mine[0], mine[1:]


def solution(mesh):
    placed = (
        P(AXES, None),
        P(AXES, None),
        P("group", "member", None),
        P("group", "member"),
        P(),
        P(),
    )
    return jax.shard_map(
        local,
        mesh=mesh,
        in_specs=placed,
        out_specs=(P(AXES), P(None, AXES)),
        check_vma=False,
    )
```

time: 95.9 us -> 80.5 us (0.84)
  the two profiles are of different devices: /device:TPU:8 before, /device:TPU:2 now
where the time goes in v2:
time: 80.5 us; the launch traced here: 80.2 us
  Pallas kernels  75 us (93%)
  local copies, waits for them, and re-layouts  4.51 us (6%)
    pallas_call x1, Pallas kernels, local(): pl.pallas_call(kernel, out_shape=jax.ShapeDtypeStruct(piece, f32), in_spe...  75 us
    unnamed x11, local copies, waits for them, and re-layouts  3.32 us

profile of v2, /device:TPU:2, one launch (start us, length us, event | category | flops | bytes accessed | tf_op | source)
XLA Modules:
  0.0 80.2 jit_solution(15384643927558934587)
XLA Ops:
  0.6 0.0 copy-start.1
  0.6 0.8 copy.9
  1.4 0.0 copy-start.3
  1.4 0.0 copy-start.4
  1.5 0.1 copy-done.1
  1.5 0.6 copy-done.3
  2.1 0.0 copy-done.4
  2.1 0.0 copy-start
  2.1 1.1 %copy-done = f32[4,64,768]{2,1,0:T(8,128)S(1)} copy-done((f32[4,64,768]{2,1,0:T(8,128)S(1)}, f32[4,64,768]{2,1,0:T(8,128)}, u32[]{:S(2)}) %copy-start) | copy-done | bytes 786456
  3.3 0.0 copy-start.2
  3.3 0.7 copy-done.2
  4.0 75.0 %search.1 = f32[4,256]{1,0:T(4,128)S(1)} custom-call(f32[8,768]{1,0:T(8,128)S(1)} %copy-done.2, f32[32,768]{1,0:T(8,128)S(1)} %copy-done.1, f32[256,768]{1,0:T(8,128)S(1)} %bitcast.4, s32[4,64]{1,0:T(4,128)S(1)} %copy-done.3, s32[1,64]{1,0:T(1,128)S(1)} %bitcast.5, s32[48,16]{1,0:T(8,128)S(1)} %reshape.15.probes), custom_call_target="tpu_custom_call" | custom-call | tf_op jit(solution)/shard_map/search/pallas_call | solution.py:316
  79.1 0.1 constant_dynamic-slice_fusion
  79.1 0.5 slice_bitcast_fusion
  79.7 0.6 slice.7
  (1 shorter events, 0.0 us)
Async XLA Ops:
  0.6 0.9 %copy-start.1 = (f32[32,768]{1,0:T(8,128)S(1)}, f32[32,768]{1,0:T(8,128)}, u32[]{:S(2)}) copy-start(f32[32,768]{1,0:T(8,128)} %cent.1) | copy-start | bytes 294916
  1.4 0.7 copy-start.3
  1.4 0.7 copy-start.4
  2.1 1.1 %copy-start = (f32[4,64,768]{2,1,0:T(8,128)S(1)}, f32[4,64,768]{2,1,0:T(8,128)}, u32[]{:S(2)}) copy-start(f32[4,64,768]{2,1,0:T(8,128)} %param.8) | copy-start | bytes 2359300
  3.3 0.7 copy-start.2

commit v3 on v2

--- a/solution.py
+++ b/solution.py
@@ -1,3 +1,5 @@
+import heapq
+
 import jax
 import jax.numpy as jnp
 from jax import lax
@@ -13,7 +15,8 @@
 PART = D // 3
 SIZES = (NX, NY, NZ)
 X, Y, Z = 0, 1, 2
-ORDERS = ((X, Y, Z), (Y, Z, X), (Z, X, Y))
+ORDERS = ((Y, X, Z), (Y, Z, X), (Z, X, Y))
+RATE, HOP, START = 46000.0, 0.8, 0.9
 VMEM_SPEC = pl.BlockSpec(memory_space=pltpu.VMEM)
 
 
@@ -48,7 +51,7 @@
     pl.semaphore_wait(barrier, len(peers))
 
 
-def kernel(q, cent, stored, ids, home, probes, best, out, cent_in, stored_in, ids_in, high, low, base, pick, acc,
+def kernel(q, cent_hbm, stored_hbm, ids_hbm, home_hbm, probes_hbm, best, out, cent, stored, ids, home, probes, cent_in, stored_in, ids_in, high, low, base, pick, acc,
            partial, from_z, from_x, from_y, mid_z, mid_x, sends, recvs, local_sems):
     at, core = place()
     group = lax.axis_index("group")
@@ -91,75 +94,116 @@
     def columns(part):
         return q.at[:, pl.ds(part * PART, PART)]
 
-    firsts = []
-    for part, order in enumerate(ORDERS):
+    own = []
+    for part in range(3):
+        own.append(pltpu.make_async_copy(columns(part), out.at[part, at[Z], at[Y], at[X]], local_sems.at[part]))
+    loads = [
+        pltpu.make_async_copy(stored_hbm, stored, local_sems.at[3]),
+        pltpu.make_async_copy(cent_hbm, cent, local_sems.at[4]),
+        pltpu.make_async_copy(ids_hbm, ids, local_sems.at[5]),
+    ]
+
+    tables = [
+        pltpu.make_async_copy(home_hbm, home, local_sems.at[6]),
+        pltpu.make_async_copy(probes_hbm, probes, local_sems.at[7]),
+    ]
+
+    events = []
+    free = {}
+    count = [0]
+
+    def at_time(when, action):
+        count[0] += 1
+        heapq.heappush(events, (when, count[0], action))
+
+    def link(now, axis, way, size):
+        done = max(now, free.get((axis, way), 0.0)) + size / RATE
+        free[axis, way] = done
+        return done + HOP + START
+
+    def index(axis, offset):
+        return lax.rem(at[axis] + (offset + SIZES[axis]), SIZES[axis])
+
+    def chunk(part, b, c, half=None):
+        span = slice(None) if half is None else pl.ds(4 * half, 4)
+        if part == 0:
+            return out.at[0, c, span, b]
+        if part == 1:
+            return out.at[1, b, span, c]
+        return out.at[2, span, c, b]
+
+    chunk_bytes = 8 * 8 * PART * 4
+    left = {}
+    swaps = []
+
+    def run_part(part):
+        first, second, third = ORDERS[part]
+        turns = [0]
+        for d in range(1, SIZES[second] // 2):
+            turns += [-d, d]
+        turns.append(SIZES[second] // 2)
+
+        def last_hop(b_off, way, step, now):
+            if step == SIZES[third] // 2 and (turns.index(b_off) % 2 == 0) != (way == 1):
+                return
+            sem = new_sem()
+            piece = chunk(part, index(second, b_off), index(third, -way * (step - 1)))
+            started.append(send(piece, piece, device(moved(at, third, way), core), sem))
+
+            def take(when):
+                arrived(chunk(part, index(second, b_off), index(third, -way * step)), sem)
+                if step < SIZES[third] // 2:
+                    last_hop(b_off, way, step + 1, when)
+                left[part, step] -= 1
+                if part == 0 and left[part, step] == 0:
+                    filled(step - 1)
+
+            at_time(link(now, third, way, chunk_bytes), take)
+
+        def have(b_off, now):
+            for way in (1, -1):
+                last_hop(b_off, way, 1, now)
+
+        def middle_hop(way, step, now):
+            last = step == SIZES[second] // 2
+            half = None if not last else (0 if way == 1 else 1)
+            sem = new_sem()
+            piece = chunk(part, index(second, -way * (step - 1)), at[third], half)
+            started.append(send(piece, piece, device(moved(at, second, way), core), sem))
+
+            def take(when):
+                arrived(chunk(part, index(second, -way * step), at[third], half), sem)
+                if not last:
+                    middle_hop(way, step + 1, when)
+                    have(-way * step, when)
+                else:
+                    left[part, "middle"] -= 1
+                    if left[part, "middle"] == 0:
+                        have(step, when)
+
+            at_time(link(now, second, way, chunk_bytes // 2 if last else chunk_bytes), take)
+
+        left[part, "middle"] = 2
+        for step in range(1, SIZES[third] // 2 + 1):
+            left[part, step] = SIZES[second] * (1 if step == SIZES[third] // 2 else 2)
+
         mine = []
-        for d in range(1, SIZES[order[0]]):
+        for d in range(1, SIZES[first]):
             sem = new_sem()
             slot = out.at[part, at[Z], at[Y], at[X]]
-            started.append(send(columns(part), slot, device(moved(at, order[0], d), core), sem))
-            fx, fy, fz = moved(at, order[0], -d)
+            started.append(send(columns(part), slot, device(moved(at, first, d), core), sem))
+            fx, fy, fz = moved(at, first, -d)
             mine.append((out.at[part, fz, fy, fx], sem))
-        firsts.append(mine)
-    own = []
-    for part in range(3):
-        copy = pltpu.make_async_copy(columns(part), out.at[part, at[Z], at[Y], at[X]], local_sems.at[part])
-        copy.start()
-        own.append(copy)
-    swaps = []
-    for src, dst in ((stored, stored_in), (cent, cent_in), (ids, ids_in)):
-        sem = new_sem()
-        started.append(send(src, dst, partner, sem))
-        swaps.append((dst, sem))
-
-    def slab(part, phase, pos, half):
-        x, y, z = at
-        first = pl.ds(0 if half == 0 else (2 if (part, phase) == (0, 1) else 4), 2 if (part, phase) == (0, 1) else 4)
-        if part == 0:
-            return out.at[0, z, pos, first] if phase == 1 else out.at[0, pos, first]
-        if part == 1:
-            return out.at[1, pos, first, x] if phase == 1 else out.at[1, first, :, pos]
-        return out.at[2, first, y, pos] if phase == 1 else out.at[2, first, pos]
-
-    def ring(part, phase, filled=None):
-        axis = ORDERS[part][phase]
-        size = SIZES[axis]
-        last = size // 2
-        streams = []
-        for way in (1, -1):
-            for turn in (0, 1):
-                half = turn if way == 1 else 1 - turn
-                hops = last if turn == 0 else last - 1
-                streams.append((way, turn, half, hops, [new_sem() for _ in range(hops)]))
-
-        def pos(offset):
-            return lax.rem(at[axis] + (offset + size), size)
-
-        def hop(stream, step):
-            way, turn, half, hops, sems = stream
-            piece = slab(part, phase, pos(-way * step), half)
-            started.append(send(piece, piece, device(moved(at, axis, way), core), sems[step]))
-
-        def take(stream, step):
-            way, turn, half, hops, sems = stream
-            arrived(slab(part, phase, pos(-way * (step + 1)), half), sems[step])
-
-        for turn in (0, 1):
-            for stream in streams:
-                if stream[1] == turn:
-                    hop(stream, 0)
-        if size == NX:
-            yield
-        for step in range(last):
-            for turn in (0, 1):
-                yield
-                for stream in streams:
-                    if stream[1] == turn and step < stream[3]:
-                        take(stream, step)
-                        if step + 1 < stream[3]:
-                            hop(stream, step + 1)
-            if filled is not None:
-                filled(step)
+
+        def take(when):
+            own[part].wait()
+            for slot, sem in mine:
+                arrived(slot, sem)
+            for way in (1, -1):
+                middle_hop(way, 1, when)
+            have(0, when)
+
+        at_time(START + HOP * SIZES[first] // 2 + 0.001 * part, take)
 
     def dot(a, b):
         return lax.dot_general(a, b, (((1,), (1,)), ((), ())), preferred_element_type=jnp.float32)
@@ -172,7 +216,9 @@
         v_low = low[:, part * PART : (part + 1) * PART]
         return dot(v_high, rhs_high) + (dot(v_high, rhs_low) + dot(v_low, rhs_high))
 
-    def prepare_vectors():
+    def prepare_vectors(when):
+        for copy in loads:
+            copy.wait()
         for slot, sem in swaps:
             arrived(slot, sem)
         start = 0
@@ -193,17 +239,18 @@
         base[2 * rows :, :] = jnp.zeros((2 * cents, width), jnp.float32)
 
     def prepare_picks():
+        for copy in tables:
+            copy.wait()
         at_slot = lax.broadcasted_iota(jnp.int32, home.shape, 1)
-        row = lax.broadcasted_iota(jnp.int32, (probes.shape[0], width), 0)
-        y_of = lax.broadcasted_iota(jnp.int32, (probes.shape[0], width), 1) // (NX * 8)
+        row = lax.broadcasted_iota(jnp.int32, (probes.shape[1], width), 0)
+        y_of = lax.broadcasted_iota(jnp.int32, (probes.shape[1], width), 1) // (NX * 8)
         for i in range(lists):
             held = jnp.max(jnp.where(home[...] == group * lists + i, at_slot, -1), axis=1, keepdims=True)
-            hit = jnp.where(probes[...] == held, jnp.float32(0), jnp.float32(LOW))
-            hit = jnp.max(hit, axis=1, keepdims=True)
-            for zh in range(2):
-                for s in range(STEPS):
-                    here = row == (y_of * 2 + zh) * STEPS + s
-                    line = jnp.where(here, hit, jnp.float32(LOW))
+            for s in range(STEPS):
+                hit = jnp.where(probes[s] == held, jnp.float32(0), jnp.float32(LOW))
+                hit = jnp.max(hit, axis=1, keepdims=True)
+                for zh in range(2):
+                    line = jnp.where(row == y_of * 2 + zh, hit, jnp.float32(LOW))
                     pick[zh, s * lists + i : s * lists + i + 1, :] = jnp.max(line, axis=0, keepdims=True)
 
     def first_third(begin, stride, count):
@@ -222,25 +269,19 @@
         else:
             first_third(NZ // 2, 1, 1)
 
-    def whole(part):
-        own[part].wait()
-        for slot, sem in firsts[part]:
-            arrived(slot, sem)
-        yield from ring(part, 1)
-        yield from ring(part, 2, filled if part == 0 else None)
-
+    for part in (1, 2, 0):
+        run_part(part)
+    for copy in own + tables + loads:
+        copy.start()
+    for src, dst in ((stored_hbm, stored_in), (cent_hbm, cent_in), (ids_hbm, ids_in)):
+        sem = new_sem()
+        started.append(send(src, dst, partner, sem))
+        swaps.append((dst, sem))
     prepare_picks()
-    running = [whole(0), whole(2), whole(1)]
-    turns = 0
-    while running:
-        for item in list(running):
-            try:
-                next(item)
-            except StopIteration:
-                running.remove(item)
-        turns += 1
-        if turns == 4:
-            prepare_vectors()
+    at_time(9.0, prepare_vectors)
+    while events:
+        when, _, action = heapq.heappop(events)
+        action(when)
 
     first_z = new_sem(NZ)
 
@@ -312,14 +353,19 @@
     width = NY * NX * 8
     piece = (1 + STEPS, width)
     held = 2 * rows + 2 * cents
-    copies = 17 + 3 + 2 * 34 + NZ + NX + NY - 2
+    copies = 21 + 3 + 16 + 80 + NZ + NX + NY - 2
     best = pl.pallas_call(
         kernel,
         out_shape=jax.ShapeDtypeStruct(piece, f32),
-        in_specs=[VMEM_SPEC] * 6,
+        in_specs=[pl.BlockSpec(memory_space=pltpu.HBM)] * 6,
         out_specs=VMEM_SPEC,
         scratch_shapes=[
             pltpu.VMEM((3, NZ, NY, NX, 8, PART), f32),
+            pltpu.VMEM((cents, D), f32),
+            pltpu.VMEM((rows, D), f32),
+            pltpu.VMEM((lists, places), jnp.int32),
+            pltpu.VMEM((1, list_home.shape[0]), jnp.int32),
+            pltpu.VMEM((STEPS, probes.shape[0], probes.shape[2]), jnp.int32),
             pltpu.VMEM((cents, D), f32),
             pltpu.VMEM((rows, D), f32),
             pltpu.VMEM((lists, places), jnp.int32),
@@ -336,11 +382,11 @@
             pltpu.VMEM(piece, f32),
             pltpu.SemaphoreType.DMA((copies,)),
             pltpu.SemaphoreType.DMA((copies,)),
-            pltpu.SemaphoreType.DMA((3,)),
+            pltpu.SemaphoreType.DMA((8,)),
         ],
-        compiler_params=pltpu.CompilerParams(collective_id=0, has_side_effects=True, vmem_limit_bytes=48 << 20),
+        compiler_params=pltpu.CompilerParams(collective_id=0, has_side_effects=True, vmem_limit_bytes=66_900_000),
         name="search",
-    )(queries, centroids, stored.reshape(rows, D), vector_ids, list_home.reshape(1, -1), probes.reshape(-1, probes.shape[2]))
+    )(queries, centroids, stored.reshape(rows, D), vector_ids, list_home.reshape(1, -1), jnp.transpose(probes, (1, 0, 2)))
     mine = lax.dynamic_slice_in_dim(best, (y * NX + x) * 8, 8, 1)
     return mine[0], mine[1:]
 

time: 80.5 us -> 78.8 us (0.979)
  local copies, waits for them, and re-layouts: 4.51 us -> 1.85 us
  Pallas kernels: 75 us -> 76.1 us
    unnamed x11 -> x0, local copies, waits for them, and re-layouts: 3.32 us -> none
    pallas_call x1, Pallas kernels: 75 us -> 76.1 us  [local(): pl.pallas_call(kernel, out_shape=jax.ShapeDtypeStruct(piece, f32), in_spe...]
where the time goes in v3:
time: 78.8 us; the launch traced here: 78.7 us
  Pallas kernels  76.1 us (97%)
  local copies, waits for them, and re-layouts  1.85 us (2%)
    pallas_call x1, Pallas kernels, local(): pl.pallas_call(kernel, out_shape=jax.ShapeDtypeStruct(piece, f32), in_spe...  76.1 us

profile of v3, /device:TPU:2, one launch (start us, length us, event | category | flops | bytes accessed | tf_op | source)
XLA Modules:
  0.0 78.7 jit_solution(9728631244028470047)
XLA Ops:
  0.7 76.1 %search.1 = f32[4,256]{1,0:T(4,128)} custom-call(f32[8,768]{1,0:T(8,128)} %q.1, f32[32,768]{1,0:T(8,128)} %cent_hbm.1, f32[256,768]{1,0:T(8,128)} %bitcast.5, s32[4,64]{1,0:T(4,128)} %ids_hbm.1, s32[1,64]{1,0:T(1,128)} %bitcast.7, s32[3,16,16]{2,1,0:T(8,128)} %bitcast.6), custom_call_target="tpu_custom_call" | custom-call | tf_op jit(solution)/shard_map/search/pallas_call | solution.py:357
  76.8 0.8 constant_dynamic-slice_fusion
  77.6 0.5 slice_bitcast_fusion
  78.1 0.6 slice.7

commit v4 on v3

--- a/solution.py
+++ b/solution.py
@@ -16,7 +16,7 @@
 SIZES = (NX, NY, NZ)
 X, Y, Z = 0, 1, 2
 ORDERS = ((Y, X, Z), (Y, Z, X), (Z, X, Y))
-RATE, HOP, START = 46000.0, 0.8, 0.9
+RATE, HOP, START = 36000.0, 0.8, 0.9
 VMEM_SPEC = pl.BlockSpec(memory_space=pltpu.VMEM)
 
 
@@ -155,8 +155,8 @@
                 if step < SIZES[third] // 2:
                     last_hop(b_off, way, step + 1, when)
                 left[part, step] -= 1
-                if part == 0 and left[part, step] == 0:
-                    filled(step - 1)
+                if left[part, step] == 0:
+                    filled(part, step, when)
 
             at_time(link(now, third, way, chunk_bytes), take)
 
@@ -238,6 +238,12 @@
                 base[first : first + places, :] = jnp.broadcast_to(column, (places, width))
         base[2 * rows :, :] = jnp.zeros((2 * cents, width), jnp.float32)
 
+        def fill(z, _):
+            acc[z] = base[...]
+            return 0
+
+        lax.fori_loop(0, NZ, fill, 0)
+
     def prepare_picks():
         for copy in tables:
             copy.wait()
@@ -253,21 +259,25 @@
                     line = jnp.where(row == y_of * 2 + zh, hit, jnp.float32(LOW))
                     pick[zh, s * lists + i : s * lists + i + 1, :] = jnp.max(line, axis=0, keepdims=True)
 
-    def first_third(begin, stride, count):
+    def add_products(part, begin, stride, count):
         def one(k, _):
             z = lax.rem(at[Z] + (begin + NZ + k * stride), NZ)
-            acc[z] = base[...] + product(0, z)
+            acc[z] += product(part, z)
             return 0
 
         lax.fori_loop(0, count, one, 0)
 
-    def filled(step):
-        if step == 0:
-            first_third(-1, 1, 3)
-        elif step < NZ // 2 - 1:
-            first_third(-(step + 1), 2 * (step + 1), 2)
-        else:
-            first_third(NZ // 2, 1, 1)
+    def filled(part, step, when):
+        if part == 0:
+            if step == 1:
+                add_products(0, -1, 1, 3)
+            elif step < NZ // 2:
+                add_products(0, -step, 2 * step, 2)
+            else:
+                add_products(0, NZ // 2, 1, 1)
+        elif all(left[part, n] == 0 for n in range(1, SIZES[ORDERS[part][2]] // 2 + 1)):
+            for n in range(0, NZ, 2):
+                at_time(when + 0.4 * n, lambda _, n=n: add_products(part, n, 1, 2))
 
     for part in (1, 2, 0):
         run_part(part)
@@ -304,13 +314,13 @@
             z_copy(distance(k - 1)).start()
 
         z = lax.rem(at[Z] + distance(k), NZ)
-        total = acc[z] + (product(1, z) + product(2, z))
+        total = acc.at[z]
         tops = []
         for i in range(lists):
-            a = jnp.max(total[i * places : (i + 1) * places], axis=0, keepdims=True)
-            b = jnp.max(total[rows + i * places : rows + (i + 1) * places], axis=0, keepdims=True)
+            a = jnp.max(total[i * places : (i + 1) * places, :], axis=0, keepdims=True)
+            b = jnp.max(total[rows + i * places : rows + (i + 1) * places, :], axis=0, keepdims=True)
             tops.append(jnp.maximum(a, b))
-        partial[z, 0:1, :] = jnp.max(total[2 * rows :], axis=0, keepdims=True)
+        partial[z, 0:1, :] = jnp.max(total[2 * rows :, :], axis=0, keepdims=True)
         chosen = pick[z // ZL]
         for s in range(STEPS):
             top = tops[0] + chosen[s * lists : s * lists + 1, :]

time: 78.8 us -> 81.5 us (1.034)
  Pallas kernels: 76.1 us -> 78.8 us
    pallas_call x1, Pallas kernels: 76.1 us -> 78.8 us  [local(): pl.pallas_call(kernel, out_shape=jax.ShapeDtypeStruct(piece, f32), in_spe...]
where the time goes in v4:
time: 81.5 us; the launch traced here: 81.3 us
  Pallas kernels  78.8 us (97%)
  local copies, waits for them, and re-layouts  1.85 us (2%)
    pallas_call x1, Pallas kernels, local(): pl.pallas_call(kernel, out_shape=jax.ShapeDtypeStruct(piece, f32), in_spe...  78.8 us

profile of v4, /device:TPU:2, one launch (start us, length us, event | category | flops | bytes accessed | tf_op | source)
XLA Modules:
  0.0 81.3 jit_solution(15320819673566290111)
XLA Ops:
  0.7 78.8 %search.1 = f32[4,256]{1,0:T(4,128)} custom-call(f32[8,768]{1,0:T(8,128)} %q.1, f32[32,768]{1,0:T(8,128)} %cent_hbm.1, f32[256,768]{1,0:T(8,128)} %bitcast.5, s32[4,64]{1,0:T(4,128)} %ids_hbm.1, s32[1,64]{1,0:T(1,128)} %bitcast.7, s32[3,16,16]{2,1,0:T(8,128)} %bitcast.6), custom_call_target="tpu_custom_call" | custom-call | tf_op jit(solution)/shard_map/search/pallas_call | solution.py:367
  79.5 0.8 constant_dynamic-slice_fusion
  80.2 0.5 slice_bitcast_fusion
  80.8 0.6 slice.7

commit v5 on v4

--- a/solution.py
+++ b/solution.py
@@ -51,7 +51,7 @@
     pl.semaphore_wait(barrier, len(peers))
 
 
-def kernel(q, cent_hbm, stored_hbm, ids_hbm, home_hbm, probes_hbm, best, out, cent, stored, ids, home, probes, cent_in, stored_in, ids_in, high, low, base, pick, acc,
+def kernel(q, cent_hbm, stored_hbm, ids_hbm, home_hbm, probes_hbm, best, out, out_z, cent, stored, ids, home, probes, cent_in, stored_in, ids_in, high, low, base, pick, acc,
            partial, from_z, from_x, from_y, mid_z, mid_x, sends, recvs, local_sems):
     at, core = place()
     group = lax.axis_index("group")
@@ -94,9 +94,12 @@
     def columns(part):
         return q.at[:, pl.ds(part * PART, PART)]
 
+    def rows_of(part, x, y, z):
+        return out_z.at[x, y, z] if part == 2 else out.at[part, z, x, y]
+
     own = []
     for part in range(3):
-        own.append(pltpu.make_async_copy(columns(part), out.at[part, at[Z], at[Y], at[X]], local_sems.at[part]))
+        own.append(pltpu.make_async_copy(columns(part), rows_of(part, *at), local_sems.at[part]))
     loads = [
         pltpu.make_async_copy(stored_hbm, stored, local_sems.at[3]),
         pltpu.make_async_copy(cent_hbm, cent, local_sems.at[4]),
@@ -127,14 +130,16 @@
     def chunk(part, b, c, half=None):
         span = slice(None) if half is None else pl.ds(4 * half, 4)
         if part == 0:
-            return out.at[0, c, span, b]
+            return out.at[0, c, b, span]
         if part == 1:
-            return out.at[1, b, span, c]
-        return out.at[2, span, c, b]
+            return out.at[1, b, c, span]
+        return out_z.at[b, c, span]
 
     chunk_bytes = 8 * 8 * PART * 4
     left = {}
     swaps = []
+    later = [lambda: prepare_vectors()]
+    copies = 21 + 3 + 16 + 80
 
     def run_part(part):
         first, second, third = ORDERS[part]
@@ -190,10 +195,9 @@
         mine = []
         for d in range(1, SIZES[first]):
             sem = new_sem()
-            slot = out.at[part, at[Z], at[Y], at[X]]
+            slot = rows_of(part, *at)
             started.append(send(columns(part), slot, device(moved(at, first, d), core), sem))
-            fx, fy, fz = moved(at, first, -d)
-            mine.append((out.at[part, fz, fy, fx], sem))
+            mine.append((rows_of(part, *moved(at, first, -d)), sem))
 
         def take(when):
             own[part].wait()
@@ -209,14 +213,14 @@
         return lax.dot_general(a, b, (((1,), (1,)), ((), ())), preferred_element_type=jnp.float32)
 
     def product(part, z):
-        rhs = out[part, z].reshape(width, PART)
+        rhs = (out_z[:, :, z] if part == 2 else out[part, z]).reshape(width, PART)
         rhs_high = rhs.astype(jnp.bfloat16)
         rhs_low = (rhs - rhs_high.astype(jnp.float32)).astype(jnp.bfloat16)
         v_high = high[:, part * PART : (part + 1) * PART]
         v_low = low[:, part * PART : (part + 1) * PART]
         return dot(v_high, rhs_high) + (dot(v_high, rhs_low) + dot(v_low, rhs_high))
 
-    def prepare_vectors(when):
+    def prepare_vectors():
         for copy in loads:
             copy.wait()
         for slot, sem in swaps:
@@ -249,7 +253,7 @@
             copy.wait()
         at_slot = lax.broadcasted_iota(jnp.int32, home.shape, 1)
         row = lax.broadcasted_iota(jnp.int32, (probes.shape[1], width), 0)
-        y_of = lax.broadcasted_iota(jnp.int32, (probes.shape[1], width), 1) // (NX * 8)
+        y_of = (lax.broadcasted_iota(jnp.int32, (probes.shape[1], width), 1) // 8) % NY
         for i in range(lists):
             held = jnp.max(jnp.where(home[...] == group * lists + i, at_slot, -1), axis=1, keepdims=True)
             for s in range(STEPS):
@@ -270,14 +274,15 @@
     def filled(part, step, when):
         if part == 0:
             if step == 1:
-                add_products(0, -1, 1, 3)
+                span = (-1, 1, 3)
             elif step < NZ // 2:
-                add_products(0, -step, 2 * step, 2)
+                span = (-step, 2 * step, 2)
             else:
-                add_products(0, NZ // 2, 1, 1)
+                span = (NZ // 2, 1, 1)
+            later.append(lambda: add_products(0, *span))
         elif all(left[part, n] == 0 for n in range(1, SIZES[ORDERS[part][2]] // 2 + 1)):
             for n in range(0, NZ, 2):
-                at_time(when + 0.4 * n, lambda _, n=n: add_products(part, n, 1, 2))
+                later.append(lambda n=n: add_products(part, n, 1, 2))
 
     for part in (1, 2, 0):
         run_part(part)
@@ -288,10 +293,13 @@
         started.append(send(src, dst, partner, sem))
         swaps.append((dst, sem))
     prepare_picks()
-    at_time(9.0, prepare_vectors)
     while events:
         when, _, action = heapq.heappop(events)
         action(when)
+        if used[0] == copies and later:
+            later.pop(0)()
+    for action in later:
+        action()
 
     first_z = new_sem(NZ)
 
@@ -370,7 +378,8 @@
         in_specs=[pl.BlockSpec(memory_space=pltpu.HBM)] * 6,
         out_specs=VMEM_SPEC,
         scratch_shapes=[
-            pltpu.VMEM((3, NZ, NY, NX, 8, PART), f32),
+            pltpu.VMEM((2, NZ, NX, NY, 8, PART), f32),
+            pltpu.VMEM((NX, NY, NZ, 8, PART), f32),
             pltpu.VMEM((cents, D), f32),
             pltpu.VMEM((rows, D), f32),
             pltpu.VMEM((lists, places), jnp.int32),
@@ -397,7 +406,7 @@
         compiler_params=pltpu.CompilerParams(collective_id=0, has_side_effects=True, vmem_limit_bytes=66_900_000),
         name="search",
     )(queries, centroids, stored.reshape(rows, D), vector_ids, list_home.reshape(1, -1), jnp.transpose(probes, (1, 0, 2)))
-    mine = lax.dynamic_slice_in_dim(best, (y * NX + x) * 8, 8, 1)
+    mine = lax.dynamic_slice_in_dim(best, (x * NY + y) * 8, 8, 1)
     return mine[0], mine[1:]
 
 

time: 81.5 us -> 84.8 us (1.040)
  Pallas kernels: 78.8 us -> 82.1 us
    pallas_call x1, Pallas kernels: 78.8 us -> 82.1 us  [local(): pl.pallas_call(kernel, out_shape=jax.ShapeDtypeStruct(piece, f32), in_spe...]
where the time goes in v5:
time: 84.8 us; the launch traced here: 84.6 us
  Pallas kernels  82.1 us (97%)
  local copies, waits for them, and re-layouts  1.85 us (2%)
    pallas_call x1, Pallas kernels, local(): pl.pallas_call(kernel, out_shape=jax.ShapeDtypeStruct(piece, f32), in_spe...  82.1 us

profile of v5, /device:TPU:2, one launch (start us, length us, event | category | flops | bytes accessed | tf_op | source)
XLA Modules:
  0.0 84.6 jit_solution(13852902844312619028)
XLA Ops:
  0.7 82.1 %search.1 = f32[4,256]{1,0:T(4,128)} custom-call(f32[8,768]{1,0:T(8,128)} %q.1, f32[32,768]{1,0:T(8,128)} %cent_hbm.1, f32[256,768]{1,0:T(8,128)} %bitcast.5, s32[4,64]{1,0:T(4,128)} %ids_hbm.1, s32[1,64]{1,0:T(1,128)} %bitcast.7, s32[3,16,16]{2,1,0:T(8,128)} %bitcast.6), custom_call_target="tpu_custom_call" | custom-call | tf_op jit(solution)/shard_map/search/pallas_call | solution.py:375
  82.8 0.8 constant_dynamic-slice_fusion
  83.5 0.5 slice_bitcast_fusion
  84.0 0.6 slice.7

commit v6 on v4

--- a/solution.py
+++ b/solution.py
@@ -16,7 +16,7 @@
 SIZES = (NX, NY, NZ)
 X, Y, Z = 0, 1, 2
 ORDERS = ((Y, X, Z), (Y, Z, X), (Z, X, Y))
-RATE, HOP, START = 36000.0, 0.8, 0.9
+RATE, HOP, START = 46000.0, 0.8, 0.9
 VMEM_SPEC = pl.BlockSpec(memory_space=pltpu.VMEM)
 
 
@@ -238,12 +238,6 @@
                 base[first : first + places, :] = jnp.broadcast_to(column, (places, width))
         base[2 * rows :, :] = jnp.zeros((2 * cents, width), jnp.float32)
 
-        def fill(z, _):
-            acc[z] = base[...]
-            return 0
-
-        lax.fori_loop(0, NZ, fill, 0)
-
     def prepare_picks():
         for copy in tables:
             copy.wait()
@@ -259,25 +253,28 @@
                     line = jnp.where(row == y_of * 2 + zh, hit, jnp.float32(LOW))
                     pick[zh, s * lists + i : s * lists + i + 1, :] = jnp.max(line, axis=0, keepdims=True)
 
-    def add_products(part, begin, stride, count):
+    groups = ((-1, 1, 3), (-2, 4, 2), (-3, 6, 2), (NZ // 2, 1, 1))
+
+    def add_products(part, group_at):
+        begin, stride, count = groups[group_at]
+
         def one(k, _):
             z = lax.rem(at[Z] + (begin + NZ + k * stride), NZ)
-            acc[z] += product(part, z)
+            acc[z] = (base[...] if part == 0 else acc[z]) + product(part, z)
             return 0
 
         lax.fori_loop(0, count, one, 0)
+
+    ready = set()
+    later = []
+    copies = 21 + 3 + 16 + 80
 
     def filled(part, step, when):
         if part == 0:
-            if step == 1:
-                add_products(0, -1, 1, 3)
-            elif step < NZ // 2:
-                add_products(0, -step, 2 * step, 2)
-            else:
-                add_products(0, NZ // 2, 1, 1)
+            add_products(0, step - 1)
+            ready.add(step - 1)
         elif all(left[part, n] == 0 for n in range(1, SIZES[ORDERS[part][2]] // 2 + 1)):
-            for n in range(0, NZ, 2):
-                at_time(when + 0.4 * n, lambda _, n=n: add_products(part, n, 1, 2))
+            later.extend((n, part) for n in range(len(groups)))
 
     for part in (1, 2, 0):
         run_part(part)
@@ -292,6 +289,13 @@
     while events:
         when, _, action = heapq.heappop(events)
         action(when)
+        if used[0] == copies:
+            able = [item for item in later if item[0] in ready]
+            if able:
+                later.remove(able[0])
+                add_products(able[0][1], able[0][0])
+    for n, part in later:
+        add_products(part, n)
 
     first_z = new_sem(NZ)
 

time: 81.5 us -> 80.7 us (level)
  no operation moved by 1% of the time
where the time goes in v6:
time: 80.7 us; the launch traced here: 80.5 us
  Pallas kernels  78 us (97%)
  local copies, waits for them, and re-layouts  1.85 us (2%)
    pallas_call x1, Pallas kernels, local(): pl.pallas_call(kernel, out_shape=jax.ShapeDtypeStruct(piece, f32), in_spe...  78 us

profile of v6, /device:TPU:2, one launch (start us, length us, event | category | flops | bytes accessed | tf_op | source)
XLA Modules:
  0.0 80.5 jit_solution(10703412312863855688)
XLA Ops:
  0.7 78.0 %search.1 = f32[4,256]{1,0:T(4,128)} custom-call(f32[8,768]{1,0:T(8,128)} %q.1, f32[32,768]{1,0:T(8,128)} %cent_hbm.1, f32[256,768]{1,0:T(8,128)} %bitcast.5, s32[4,64]{1,0:T(4,128)} %ids_hbm.1, s32[1,64]{1,0:T(1,128)} %bitcast.7, s32[3,16,16]{2,1,0:T(8,128)} %bitcast.6), custom_call_target="tpu_custom_call" | custom-call | tf_op jit(solution)/shard_map/search/pallas_call | solution.py:371
  78.7 0.8 constant_dynamic-slice_fusion
  79.4 0.5 slice_bitcast_fusion
  80.0 0.6 slice.7

commit v7 on v3

--- a/solution.py
+++ b/solution.py
@@ -387,8 +387,8 @@
         compiler_params=pltpu.CompilerParams(collective_id=0, has_side_effects=True, vmem_limit_bytes=66_900_000),
         name="search",
     )(queries, centroids, stored.reshape(rows, D), vector_ids, list_home.reshape(1, -1), jnp.transpose(probes, (1, 0, 2)))
-    mine = lax.dynamic_slice_in_dim(best, (y * NX + x) * 8, 8, 1)
-    return mine[0], mine[1:]
+    first = (y * NX + x) * 8
+    return lax.dynamic_slice(best, (0, first), (1, 8)).reshape(8), lax.dynamic_slice(best, (1, first), (STEPS, 8))
 
 
 def solution(mesh):

time: 78.8 us -> 79.6 us (1.010)
    reshape x0 -> x1, local copies, waits for them, and re-layouts: none -> 1.27 us  [local(): lax.dynamic_slice(best, (0, first), (1, 8)).reshape(8)]
where the time goes in v7:
time: 79.6 us; the launch traced here: 79.4 us
  Pallas kernels  76.1 us (96%)
  local copies, waits for them, and re-layouts  2.6 us (3%)
    pallas_call x1, Pallas kernels, local(): pl.pallas_call(kernel, out_shape=jax.ShapeDtypeStruct(piece, f32), in_spe...  76.1 us

profile of v7, /device:TPU:2, one launch (start us, length us, event | category | flops | bytes accessed | tf_op | source)
XLA Modules:
  0.0 79.4 jit_solution(187719769369576762)
XLA Ops:
  0.7 76.1 %search.1 = f32[4,256]{1,0:T(4,128)} custom-call(f32[8,768]{1,0:T(8,128)} %q.1, f32[32,768]{1,0:T(8,128)} %cent_hbm.1, f32[256,768]{1,0:T(8,128)} %bitcast.5, s32[4,64]{1,0:T(4,128)} %ids_hbm.1, s32[1,64]{1,0:T(1,128)} %bitcast.7, s32[3,16,16]{2,1,0:T(8,128)} %bitcast.6), custom_call_target="tpu_custom_call" | custom-call | tf_op jit(solution)/shard_map/search/pallas_call | solution.py:357
  76.8 1.3 %dynamic-slice_bitcast_fusion = f32[8]{0:T(128)} fusion(f32[4,256]{1,0:T(4,128)} %search.1, s32[]{:T(128)S(6)} %select_n.21), kind=kLoop, calls=%fused_computation | loop fusion | bytes 68 | tf_op jit(solution)/shard_map/reshape | solution.py:391
  78.1 1.3 %constant_dynamic-slice_fusion = f32[3,8]{1,0:T(4,128)} fusion(f32[4,256]{1,0:T(4,128)} %search.1, s32[]{:T(128)S(6)} %select_n.21), kind=kLoop, calls=%fused_computation.1 | loop fusion | bytes 196 | tf_op jit(solution)/shard_map/dynamic_slice | solution.py:391
